TPU v7x, 32 devices: a whole 2x2x4 slice. The times are simulated.
32 devices in a mesh: groups: 2 (over y), sess: 4 (over z), inner: 2 (over x), rep: 2 (over core).
Axes of the slice: x: 2, y: 2, z: 4, core: 2. Of those that a mesh axis runs over, the one named last changes fastest.
Arguments:
- thinker_rows: bfloat16 [4096, 3584], P(('groups', 'sess', 'rep'), 'inner'), parts along dimension 0, may hold values from -6 to 6
- row_session: int32 [4096, 1], P(('groups', 'sess', 'rep')), parts along dimension 0, may hold values from 0 to 31; in each aligned block of 256 rows (0 to 255, 256 to 511, ...) at most 12 rows name the same one
- speaker_of: int32 [64], P('groups'), parts along dimension 0, may hold values from 0 to 7
- prompt_slot: int32 [16], P('groups'), parts along dimension 0, may hold values from 0 to 7, each once
- prompt_cache: bfloat16 [16, 1024, 1024], P(('groups', 'sess'), ('inner', 'rep')), parts along dimension 0, may hold values from -64 to 64
- proj_weight: bfloat16 [3584, 896], P('inner'), may hold values from -0.09375 to 0.09375
- attn_gain: bfloat16 [896], replicated, may hold values from 0.5 to 1.5
- q_weight: bfloat16 [896, 1536], replicated, may hold values from -0.1875 to 0.1875
- k_weight: bfloat16 [896, 512], replicated, may hold values from -0.625 to 0.625
- v_weight: bfloat16 [896, 512], replicated, may hold values from -0.1875 to 0.1875
- o_weight: bfloat16 [1536, 896], replicated, may hold values from -0.15625 to 0.15625
Outputs:
- voice_states: bfloat16 [64, 96, 896], P(('groups', 'sess', 'inner', 'rep')), parts along dimension 0
There are 2 independent parts, one for each index of `groups`. A program takes and returns all parts, laid end to end along the dimension named above; an argument that names none is the same for every part. Nothing has to cross between parts.
Inputs may be any that keep to these rules, and one draw needn't show every extreme that they name: `row_session`: column 0 names the session of the row. Within each block of 256 rows (rows b * 256 to (b + 1) * 256 - 1, the rows of one index of sess+rep) no session is named by more than 12 rows, a bound that some block reaches; every session is named by some row. `prompt_slot`: each slot holds exactly one speaker's prompt.
All inputs are finite; a program needn't handle non-finite values.
Results may differ from a plain program's by a relative error of at most 0.0071.
Values may be sent and summed in bfloat16 or wider, within the bound.
No kernel may reach another device: no remote copies, remote signals or barrier semaphores. Data moves between devices by JAX's collectives and lax.ppermute only.
A program may use at most 128 MiB of HBM per device.

v0:
```python
import jax
import jax.numpy as jnp
from jax import lax
from jax.sharding import PartitionSpec as P

H = 12
KVH = 4
HD = 128
PROMPT = 1024
SLOTS = 96
EPSILON = 1e-06
ROPE_BASE = 1000000.0


def rms_scale(states, gain):
    widened = states.astype(jnp.float32)
    factor = lax.rsqrt(jnp.mean(widened * widened, axis=-1, keepdims=True) + EPSILON)
    return (widened * factor * gain.astype(jnp.float32)).astype(jnp.bfloat16)


def rope_tables(slot_total):
    half_width = HD // 2
    inverse = ROPE_BASE ** (-(jnp.arange(half_width, dtype=jnp.float32) * 2.0) / HD)
    angles = (PROMPT + jnp.arange(slot_total)).astype(jnp.float32)[:, None] * inverse[None, :]
    cosine = jnp.concatenate([jnp.cos(angles), jnp.cos(angles)], axis=1)[:, None, :]
    sine_table = jnp.concatenate([jnp.sin(angles), jnp.sin(angles)], axis=1)[:, None, :]
    return (cosine, sine_table)


def rotate(vectors, cosine, sine_table):
    half_width = vectors.shape[-1] // 2
    turned = jnp.concatenate([-vectors[..., half_width:], vectors[..., :half_width]], axis=-1)
    return vectors * cosine + turned * sine_table


def attend(states, lengths, prompts, attn_gain, q_weight, k_weight, v_weight, o_weight):
    session_total, slot_total, model_width = states.shape
    flat_rows = states.reshape(session_total * slot_total, model_width)
    normed = rms_scale(flat_rows, attn_gain)
    cosine, sine_table = rope_tables(slot_total)
    query = rotate(
        jnp.dot(normed, q_weight, preferred_element_type=jnp.float32).reshape(
            session_total, slot_total, H, HD
        ),
        cosine,
        sine_table,
    ).astype(jnp.bfloat16)
    own_keys = rotate(
        jnp.dot(normed, k_weight, preferred_element_type=jnp.float32).reshape(
            session_total, slot_total, KVH, HD
        ),
        cosine,
        sine_table,
    ).astype(jnp.bfloat16)
    own_values = (
        jnp.dot(normed, v_weight, preferred_element_type=jnp.float32)
        .reshape(session_total, slot_total, KVH, HD)
        .astype(jnp.bfloat16)
    )
    prompt_keys = prompts[:, :, : KVH * HD].reshape(session_total, PROMPT, KVH, HD)
    prompt_values = prompts[:, :, KVH * HD :].reshape(session_total, PROMPT, KVH, HD)
    all_keys = jnp.concatenate([prompt_keys, own_keys], axis=1)
    all_values = jnp.concatenate([prompt_values, own_values], axis=1)
    key_place = jnp.arange(PROMPT + slot_total) - PROMPT
    query_place = jnp.arange(slot_total)
    allowed = (key_place[None, None, :] < 0) | (
        key_place[None, None, :] <= query_place[None, :, None]
    ) & (key_place[None, None, :] < lengths[:, None, None])
    per_group = H // KVH
    outputs = []
    for kv_head in range(KVH):
        query_group = query[:, :, kv_head * per_group : (kv_head + 1) * per_group]
        scores = jnp.einsum(
            "cqhd,ckd->chqk",
            query_group,
            all_keys[:, :, kv_head],
            preferred_element_type=jnp.float32,
        ) * HD ** (-0.5)
        scores = jnp.where(allowed[:, None], scores, -1e30)
        highest = jnp.max(scores, axis=-1, keepdims=True)
        powers = jnp.exp(scores - highest)
        weights = (powers / jnp.sum(powers, axis=-1, keepdims=True)).astype(jnp.bfloat16)
        outputs.append(
            jnp.einsum(
                "chqk,ckd->cqhd",
                weights,
                all_values[:, :, kv_head],
                preferred_element_type=jnp.float32,
            )
        )
    attended = (
        jnp.concatenate(outputs, axis=2)
        .reshape(session_total * slot_total, H * HD)
        .astype(jnp.bfloat16)
    )
    return flat_rows.astype(jnp.float32) + jnp.dot(
        attended, o_weight, preferred_element_type=jnp.float32
    )


def body(
    thinker_rows,
    row_session,
    speaker_of,
    prompt_slot,
    prompt_cache,
    proj_weight,
    attn_gain,
    q_weight,
    k_weight,
    v_weight,
    o_weight,
):
    sess_count = lax.axis_size("sess")
    inner_count = lax.axis_size("inner")
    rep_count = lax.axis_size("rep")
    owner_count = sess_count * rep_count
    session_all = speaker_of.shape[0]
    per_device = session_all // (owner_count * inner_count)
    per_owner = per_device * inner_count
    slot_cap = SLOTS // owner_count
    inner_place = lax.axis_index("inner")
    shard_place = lax.axis_index("sess")
    row_owner = row_session[:, 0]
    device_of = row_owner // per_device
    target = (
        (device_of // (inner_count * rep_count) * rep_count + device_of % rep_count) * per_owner
        + device_of // rep_count % inner_count * per_device
        + row_owner % per_device
    )
    row_order = jnp.arange(row_owner.shape[0])
    earlier = jnp.sum(
        (
            (row_owner[:, None] == row_owner[None, :]) & (row_order[None, :] < row_order[:, None])
        ).astype(jnp.int32),
        axis=1,
    )
    slot_place = target * slot_cap + earlier
    counts = jnp.sum(
        (target[:, None] == jnp.arange(owner_count * per_owner)[None, :]).astype(jnp.int32), axis=0
    ).reshape(owner_count, per_owner)
    partial_sum = jnp.dot(thinker_rows, proj_weight, preferred_element_type=jnp.float32)
    own_columns = lax.psum_scatter(partial_sum, "inner", scatter_dimension=1, tiled=True).astype(
        jnp.bfloat16
    )
    buffer = (
        jnp.zeros((owner_count * per_owner * slot_cap, own_columns.shape[1]), own_columns.dtype)
        .at[slot_place]
        .set(own_columns)
    )
    arrived = lax.all_to_all(
        buffer.reshape(owner_count, per_owner * slot_cap, own_columns.shape[1]),
        ("sess", "rep"),
        split_axis=0,
        concat_axis=0,
        tiled=True,
    )
    counts_in = lax.all_to_all(counts, ("sess", "rep"), split_axis=0, concat_axis=0, tiled=True)
    arrived_rows = arrived.reshape(owner_count, per_owner, slot_cap, arrived.shape[2])
    regrouped = lax.all_to_all(arrived_rows, "inner", split_axis=1, concat_axis=3, tiled=True)
    projected = jnp.transpose(regrouped, (1, 0, 2, 3)).reshape(
        per_device, owner_count * slot_cap, regrouped.shape[3]
    )
    own_counts = lax.dynamic_slice_in_dim(counts_in, inner_place * per_device, per_device, 1)
    offsets = jnp.cumsum(own_counts, axis=0) - own_counts
    lengths = jnp.sum(own_counts, axis=0)
    within = jnp.arange(slot_cap)
    position = jnp.transpose(offsets)[:, :, None] + within[None, None, :]
    live_slot = within[None, None, :] < jnp.transpose(own_counts)[:, :, None]
    position = jnp.where(live_slot, position, SLOTS).reshape(per_device, owner_count * slot_cap)
    session_rows = jnp.broadcast_to(jnp.arange(per_device)[:, None], position.shape)
    compact = (
        jnp.zeros((per_device, SLOTS, projected.shape[2]), jnp.bfloat16)
        .at[session_rows, position]
        .set(projected, mode="drop")
    )
    shard_sessions = per_device * inner_count * rep_count
    wanted_speaker = lax.dynamic_slice_in_dim(
        speaker_of, shard_place * shard_sessions, shard_sessions
    )
    speaker_table = jnp.arange(prompt_slot.shape[0])
    wanted_slot = jnp.sum(
        jnp.where(wanted_speaker[:, None] == speaker_table[None, :], prompt_slot[None, :], 0),
        axis=1,
    )
    piece = lax.all_gather(prompt_cache, "sess", axis=0, tiled=True)
    matching = (wanted_slot[:, None] == jnp.arange(piece.shape[0])[None, :]).astype(jnp.bfloat16)
    chosen = jnp.einsum("sp,ptc->stc", matching, piece, preferred_element_type=jnp.float32)
    prompts = lax.all_to_all(
        chosen.astype(jnp.bfloat16), ("inner", "rep"), split_axis=0, concat_axis=1, tiled=True
    )
    summed = attend(compact, lengths, prompts, attn_gain, q_weight, k_weight, v_weight, o_weight)
    live_rows = (jnp.arange(SLOTS)[None, :] < lengths[:, None]).reshape(-1, 1)
    return (
        jnp.where(live_rows, summed, 0.0)
        .astype(jnp.bfloat16)
        .reshape(per_device, SLOTS, summed.shape[1])
    )


def solution(mesh):
    in_specs = (
        P(("groups", "sess", "rep"), "inner"),
        P(("groups", "sess", "rep"), None),
        P("groups"),
        P("groups"),
        P(("groups", "sess"), ("inner", "rep"), None),
        P("inner", None),
        P(),
        P(),
        P(),
        P(),
        P(),
    )
    out_specs = P(("groups", "sess", "inner", "rep"), None, None)
    return jax.shard_map(body, mesh=mesh, in_specs=in_specs, out_specs=out_specs, check_vma=False)
```

profile of v0, /device:TPU:0, one launch (start us, length us, event | category | flops | bytes accessed | tf_op | source)
XLA Modules:
  0.0 214.4 jit_solution(5181493876565836849)
XLA Ops:
  7.4 1.9 copy-done
  9.3 3.5 %fusion.175 = f32[256,896]{0,1:T(8,128)} fusion(bf16[256,1792]{1,0:T(8,128)(2,1)} %param.11, bf16[1792,896]{1,0:T(8,128)(2,1)S(1)} %copy-done), kind=kOutput, calls=%fused_computation.189 | convolution fusion | flops 822083584 | bytes 5046272 | tf_op jit(solution)/shard_map/dot_general | solution.py:142
  12.8 0.5 all-gather.2.cloned.1.call-update
  13.4 0.2 convert_reduce_fusion
  13.6 0.1 convert_reduce_fusion.1
  13.7 0.7 all_to_all.35
  14.4 6.3 %all-to-all-start = ((s32[8,1,4]{2,1,0:T(1,128)}), s32[8,1,4]{2,1,0:T(1,128)S(1)}, u32[]{:S(2)}, u32[]{:S(2)}) async-start(s32[8,1,4]{2,1,0:T(1,128)} %bitcast.1), calls=%async_computation | async-start | bytes 8192 | tf_op jit(solution)/shard_map/all_to_all | solution.py:158
  20.7 4.9 %copy.90 = bf16[896,1536]{0,1:T(8,128)(2,1)} copy(bf16[896,1536]{1,0:T(8,128)(2,1)} %param.18) | data formatting | bytes 5505024 | tf_op args[7]
  25.7 0.6 copy.102
  26.5 0.2 select_reduce_fusion
  26.7 0.2 multiply_cosine_fusion
  26.9 0.7 pad_maximum_fusion.3
  27.7 1.3 copy.101
  29.0 0.1 fusion.152
  29.1 0.2 reduce_window_sum.11
  29.3 5.2 %reduce-scatter.2.cloned.1.call-done = f32[256,448]{0,1:T(8,128)} async-done(((f32[256,896]{0,1:T(8,128)}), f32[256,448]{0,1:T(8,128)}) %reduce-scatter.2.cloned.1.call-update) | async-done | bytes 458768 | tf_op jit(solution)/shard_map/reduce_scatter | solution.py:143
  34.5 1.0 convert_element_type.78
  35.6 0.1 copy.75
  35.7 2.2 %scatter_custom_fusion = bf16[384,448]{1,0:T(8,128)(2,1)} fusion(s32[256]{0:T(256)S(1)} %bitcast.200, bf16[256,448]{1,0:T(8,128)(2,1)S(1)} %copy.75, bf16[]{:T(256)} %constant.95.clone.1), kind=kCustom, calls=%fused_computation.98 | custom fusion | bytes 344066 | tf_op jit(solution)/shard_map/scatter | solution.py:149
  38.0 4.6 %all-to-all-start.1 = ((bf16[8,48,448]{2,1,0:T(8,128)(2,1)}), bf16[8,48,448]{2,1,0:T(8,128)(2,1)S(1)}, u32[]{:S(2)}, u32[]{:S(2)}) async-start(bf16[8,48,448]{2,1,0:T(8,128)(2,1)} %bitcast.8), calls=%async_computation.2 | async-start | bytes 786432 | tf_op jit(solution)/shard_map/all_to_all | solution.py:151
  42.7 0.1 add.150
  42.8 0.1 lt.144
  42.9 0.1 reshape.305
  43.1 0.6 lt.139
  43.7 24.4 %all-to-all-done.1 = bf16[8,48,448]{2,1,0:T(8,128)(2,1)S(1)} async-done(((bf16[8,48,448]{2,1,0:T(8,128)(2,1)}), bf16[8,48,448]{2,1,0:T(8,128)(2,1)S(1)}, u32[]{:S(2)}, u32[]{:S(2)}) %all-to-all-start.1) | async-done | bytes 344096 | tf_op jit(solution)/shard_map/all_to_all | solution.py:151
  68.1 1.0 copy.76
  69.1 3.5 %all-to-all-start.2 = ((bf16[8,4,12,448]{3,0,2,1:T(8,128)(2,1)}), bf16[8,4,12,448]{3,0,2,1:T(8,128)(2,1)S(1)}, u32[]{:S(2)}, u32[]{:S(2)}) async-start(bf16[8,4,12,448]{3,0,2,1:T(8,128)(2,1)} %bitcast.9), calls=%async_computation.3 | async-start | bytes 786432 | tf_op jit(solution)/shard_map/all_to_all | solution.py:160
  72.5 33.9 %all-gather.2.cloned.1.call-done = bf16[8,256,1024]{2,1,0:T(8,128)(2,1)} async-done(((bf16[2,256,1024]{2,1,0:T(8,128)(2,1)}), bf16[8,256,1024]{2,1,0:T(8,128)(2,1)}) %all-gather.2.cloned.1.call-update) | async-done | bytes 4194320 | tf_op jit(solution)/shard_map/all_gather | solution.py:186
  106.4 4.7 %fusion.22 = bf16[8,256,1024]{2,0,1:T(8,128)(2,1)S(1)} fusion(bf16[8,256,1024]{2,1,0:T(8,128)(2,1)} %all-gather.2.cloned.1.call-done, s32[8]{0:T(128)S(1)} %select_reduce_fusion), kind=kOutput, calls=%fused_computation.34 | convolution fusion | flops 35651648 | bytes 8388640 | tf_op jit(solution)/shard_map/sp,ptc->stc/dot_general | solution.py:188
  111.2 4.3 %copy.80 = bf16[8,256,1024]{2,1,0:T(8,128)(2,1)} copy(bf16[8,256,1024]{2,0,1:T(8,128)(2,1)S(1)} %fusion.22) | data formatting | bytes 8388608 | tf_op jit(solution)/shard_map/convert_element_type | solution.py:190
  115.4 5.0 %all-to-all-start.3 = ((bf16[8,256,1024]{2,1,0:T(8,128)(2,1)}), bf16[8,256,1024]{2,1,0:T(8,128)(2,1)}, u32[]{:S(2)}, u32[]{:S(2)}) async-start(bf16[8,256,1024]{2,1,0:T(8,128)(2,1)} %copy.80), calls=%async_computation.4 | async-start | bytes 8388608 | tf_op jit(solution)/shard_map/all_to_all | solution.py:189
  120.5 0.8 and_or_fusion
  121.4 0.4 copy.77
  121.8 0.3 all_to_all.41
  122.3 13.1 %scatter_fusion = bf16[2,96,896]{2,1,0:T(8,128)(2,1)S(1)} fusion(bf16[2,96,896]{2,1,0:T(8,128)(2,1)S(1)} %broadcast_in_dim.55, s32[192]{0:T(256)S(1)} %reshape.305, bf16[192,896]{1,0:T(8,128)(2,1)S(1)} %reshape.307), kind=kCustom, calls=%fused_computation.1 | custom fusion | bytes 1033728 | tf_op jit(solution)/shard_map/scatter | solution.py:175
  135.3 0.2 multiply_reduce_fusion
  135.5 0.5 fusion.115
  136.0 0.2 slice_negate_fusion.1
  136.2 0.9 fusion.68
  137.1 1.2 convolution_convert_fusion
  138.3 1.1 fusion.113
  139.4 0.4 slice_negate_fusion
  139.8 0.4 fusion.32
  140.3 28.3 %all-to-all-done.3 = bf16[8,256,1024]{2,1,0:T(8,128)(2,1)} async-done(((bf16[8,256,1024]{2,1,0:T(8,128)(2,1)}), bf16[8,256,1024]{2,1,0:T(8,128)(2,1)}, u32[]{:S(2)}, u32[]{:S(2)}) %all-to-all-start.3) | async-done | bytes 4194336 | tf_op jit(solution)/shard_map/all_to_all | solution.py:189
  168.5 2.6 %copy.81 = bf16[2,4,256,1024]{3,2,1,0:T(8,128)(2,1)S(1)} copy(bf16[2,4,256,1024]{3,2,0,1:T(8,128)(2,1)} %bitcast.16) | data formatting | bytes 8388608 | tf_op jit(solution)/shard_map/all_to_all | solution.py:189
  171.1 2.5 %fusion.154 = (bf16[2,1024,512]{2,1,0:T(8,128)(2,1)}, bf16[2,1024,512]{2,1,0:T(8,128)(2,1)}) fusion(bf16[2,1024,1024]{2,1,0:T(8,128)(2,1)S(1)} %bitcast.185), kind=kLoop, calls=%fused_computation.184 | loop fusion | bytes 8388608 | tf_op jit(solution)/shard_map/slice | solution.py:61
  173.6 3.0 %copy.86 = bf16[2,1024,512]{1,2,0:T(8,128)(2,1)S(1)} copy(bf16[2,1024,512]{2,1,0:T(8,128)(2,1)} %get-tuple-element.10) | data formatting | bytes 4194304 | tf_op jit(solution)/shard_map/slice | solution.py:60
  176.7 2.5 %copy.88 = bf16[2,1024,4,128]{3,1,0,2:T(8,128)(2,1)} copy(bf16[2,1024,4,128]{1,3,2,0:T(8,128)(2,1)S(1)} %bitcast.187) | data formatting | bytes 4194304 | tf_op jit(solution)/shard_map/reshape | solution.py:60
  179.2 3.8 %fusion.155 = (f32[2,3,96]{2,1,0:T(4,128)S(1)}, f32[2,3,96,1120]{3,2,1,0:T(8,128)}) fusion(pred[2,96,1120]{2,1,0:T(8,128)(4,1)S(1)} %copy-done.9, bf16[2,1024,4,128]{3,1,0,2:T(8,128)(2,1)} %copy.88, bf16[2,96,12,128]{3,1,2,0:T(8,128)(2,1)S(1)} %fusion.32, bf16[2,96,4,128]{3,1,2,0:T(8,128)(2,1)S(1)} %copy-done.10), kind=kOutput, calls=%fused_computation.185 | convolution fusion | flops 168879200 | bytes 5245184 | tf_op jit(solution)/shard_map/sub | solution.py:81
  183.0 2.6 %fusion.160 = (f32[2,3,96]{2,1,0:T(4,128)S(1)}, f32[2,3,96,1120]{3,2,1,0:T(8,128)}) fusion(pred[2,96,1120]{2,1,0:T(8,128)(4,1)S(1)} %copy-done.9, bf16[2,1024,4,128]{3,1,0,2:T(8,128)(2,1)S(1)} %copy-done.4, bf16[2,96,12,128]{3,1,2,0:T(8,128)(2,1)S(1)} %fusion.32, bf16[2,96,4,128]{3,1,2,0:T(8,128)(2,1)S(1)} %copy-done.10), kind=kOutput, calls=%fused_computation.186 | convolution fusion | flops 168879200 | bytes 5245184 | tf_op jit(solution)/shard_map/sub | solution.py:81
  185.7 2.6 %fusion.165 = (f32[2,3,96]{2,1,0:T(4,128)S(1)}, f32[2,3,96,1120]{3,2,1,0:T(8,128)}) fusion(pred[2,96,1120]{2,1,0:T(8,128)(4,1)S(1)} %copy-done.9, bf16[2,1024,4,128]{3,1,0,2:T(8,128)(2,1)S(1)} %copy-done.4, bf16[2,96,12,128]{3,1,2,0:T(8,128)(2,1)S(1)} %fusion.32, bf16[2,96,4,128]{3,1,2,0:T(8,128)(2,1)S(1)} %copy-done.10), kind=kOutput, calls=%fused_computation.187 | convolution fusion | flops 168879200 | bytes 5245184 | tf_op jit(solution)/shard_map/sub | solution.py:81
  188.3 2.7 %fusion.170 = (f32[2,3,96]{2,1,0:T(4,128)S(1)}, f32[2,3,96,1120]{3,2,1,0:T(8,128)}) fusion(pred[2,96,1120]{2,1,0:T(8,128)(4,1)S(1)} %copy-done.9, bf16[2,1024,4,128]{3,1,0,2:T(8,128)(2,1)S(1)} %copy-done.4, bf16[2,96,12,128]{3,1,2,0:T(8,128)(2,1)S(1)} %fusion.32, bf16[2,96,4,128]{3,1,2,0:T(8,128)(2,1)S(1)} %copy-done.10), kind=kOutput, calls=%fused_computation.188 | convolution fusion | flops 168879200 | bytes 5245184 | tf_op jit(solution)/shard_map/sub | solution.py:81
  190.9 3.0 %copy.82 = bf16[2,1024,512]{1,2,0:T(8,128)(2,1)S(1)} copy(bf16[2,1024,512]{2,1,0:T(8,128)(2,1)} %get-tuple-element.9) | data formatting | bytes 4194304 | tf_op jit(solution)/shard_map/slice | solution.py:61
  193.9 2.9 %copy.84 = bf16[2,1024,4,128]{3,1,0,2:T(8,128)(2,1)} copy(bf16[2,1024,4,128]{1,3,2,0:T(8,128)(2,1)S(1)} %bitcast.188) | data formatting | bytes 4194304 | tf_op jit(solution)/shard_map/reshape | solution.py:61
  196.8 2.6 %fusion.40 = bf16[2,96,3,128]{3,1,2,0:T(8,128)(2,1)S(1)} fusion(f32[2,3,96,1120]{3,2,1,0:T(8,128)} %get-tuple-element.18, f32[2,3,96]{2,1,0:T(4,128)S(1)} %get-tuple-element.17, bf16[2,1024,4,128]{3,1,0,2:T(8,128)(2,1)} %copy.84, bf16[2,96,4,128]{3,1,2,0:T(8,128)(2,1)S(1)} %copy-done.17), kind=kOutput, calls=%fused_computation.64 | convolution fusion | flops 167661568 | bytes 5024000 | tf_op jit(solution)/shard_map/chqk,ckd->cqhd/dot_general | solution.py:84
  199.4 0.7 copy-done.20
  200.1 0.6 fusion.39
  200.7 1.2 copy-done.19
  201.9 0.6 fusion.38
  202.5 1.2 copy-done.18
  203.6 0.6 fusion.37
  204.3 0.3 copy.91
  204.6 0.8 copy-done.13
  205.4 1.5 fusion.30
  (64 shorter events, 1.1 us)
Async XLA Ops:
  7.4 1.9 copy-start
  7.4 6.0 %copy-start.11 = (s32[256,1]{0,1:T(1,128)S(1)}, s32[256,1]{0,1:T(1,128)}, u32[]{:S(2)}) copy-start(s32[256,1]{0,1:T(1,128)} %param.12) | copy-start | bytes 3076
  7.4 27.1 %reduce-scatter.2.cloned.1.call-start = ((), (), s32[]{:S(2)}) async-start(), calls=%async_computation.5 | async-start | bytes 1376256 | tf_op jit(solution)/shard_map/reduce_scatter | solution.py:143
  12.8 93.7 %all-gather.2.cloned.1.call-start = ((), (), s32[]{:S(2)}) async-start(), calls=%async_computation.6 | async-start | bytes 5242880 | tf_op jit(solution)/shard_map/all_gather | solution.py:186
  14.4 14.6 %all-to-all-start = ((s32[8,1,4]{2,1,0:T(1,128)}), s32[8,1,4]{2,1,0:T(1,128)S(1)}, u32[]{:S(2)}, u32[]{:S(2)}) async-start(s32[8,1,4]{2,1,0:T(1,128)} %bitcast.1), calls=%async_computation | async-start | bytes 8192 | tf_op jit(solution)/shard_map/all_to_all | solution.py:158
  20.7 5.0 %copy-start.12 = (bf16[896]{0:T(1024)(128)(2,1)S(1)}, bf16[896]{0:T(1024)(128)(2,1)}, u32[]{:S(2)}) copy-start(bf16[896]{0:T(1024)(128)(2,1)} %param.17) | copy-start | bytes 5380
  20.7 5.0 %copy-start.5 = (bf16[896,512]{1,0:T(8,128)(2,1)S(1)}, bf16[896,512]{1,0:T(8,128)(2,1)}, u32[]{:S(2)}) copy-start(bf16[896,512]{1,0:T(8,128)(2,1)} %param.19) | copy-start | bytes 2752516
  20.7 5.6 %copy-start.14 = (s32[32]{0:T(128)S(1)}, s32[32]{0:T(128)}, u32[]{:S(2)}) copy-start(s32[32]{0:T(128)} %param.13) | copy-start | bytes 388
  20.7 5.7 %copy-start.15 = (s32[8]{0:T(128)S(1)}, s32[8]{0:T(128)}, u32[]{:S(2)}) copy-start(s32[8]{0:T(128)} %param.14) | copy-start | bytes 100
  25.6 2.1 copy-start.6
  38.0 30.1 %all-to-all-start.1 = ((bf16[8,48,448]{2,1,0:T(8,128)(2,1)}), bf16[8,48,448]{2,1,0:T(8,128)(2,1)S(1)}, u32[]{:S(2)}, u32[]{:S(2)}) async-start(bf16[8,48,448]{2,1,0:T(8,128)(2,1)} %bitcast.8), calls=%async_computation.2 | async-start | bytes 786432 | tf_op jit(solution)/shard_map/all_to_all | solution.py:151
  69.1 46.4 %all-to-all-start.2 = ((bf16[8,4,12,448]{3,0,2,1:T(8,128)(2,1)}), bf16[8,4,12,448]{3,0,2,1:T(8,128)(2,1)S(1)}, u32[]{:S(2)}, u32[]{:S(2)}) async-start(bf16[8,4,12,448]{3,0,2,1:T(8,128)(2,1)} %bitcast.9), calls=%async_computation.3 | async-start | bytes 786432 | tf_op jit(solution)/shard_map/all_to_all | solution.py:160
  115.4 53.1 %all-to-all-start.3 = ((bf16[8,256,1024]{2,1,0:T(8,128)(2,1)}), bf16[8,256,1024]{2,1,0:T(8,128)(2,1)}, u32[]{:S(2)}, u32[]{:S(2)}) async-start(bf16[8,256,1024]{2,1,0:T(8,128)(2,1)} %copy.80), calls=%async_computation.4 | async-start | bytes 8388608 | tf_op jit(solution)/shard_map/all_to_all | solution.py:189
  135.3 0.9 copy-start.8
  135.5 1.6 copy-start.7
  136.0 2.2 %copy-start.2 = (bf16[896,1536]{0,1:T(8,128)(2,1)S(1)}, bf16[896,1536]{0,1:T(8,128)(2,1)}, u32[]{:S(2)}) copy-start(bf16[896,1536]{0,1:T(8,128)(2,1)} %copy.90) | copy-start | bytes 8257540
  176.6 2.6 %copy-start.9 = (pred[2,96,1120]{2,1,0:T(8,128)(4,1)S(1)}, pred[2,96,1120]{2,1,0:T(8,128)(4,1)}, u32[]{:S(2)}) copy-start(pred[2,96,1120]{2,1,0:T(8,128)(4,1)} %and_or_fusion) | copy-start | bytes 645124
  176.6 2.6 %copy-start.10 = (bf16[2,96,4,128]{3,1,2,0:T(8,128)(2,1)S(1)}, bf16[2,96,4,128]{3,1,2,0:T(8,128)(2,1)}, u32[]{:S(2)}) copy-start(bf16[2,96,4,128]{3,1,2,0:T(8,128)(2,1)} %fusion.68) | copy-start | bytes 589828
  179.2 3.8 %copy-start.4 = (bf16[2,1024,4,128]{3,1,0,2:T(8,128)(2,1)S(1)}, bf16[2,1024,4,128]{3,1,0,2:T(8,128)(2,1)}, u32[]{:S(2)}) copy-start(bf16[2,1024,4,128]{3,1,0,2:T(8,128)(2,1)} %copy.88) | copy-start | bytes 6291460
  193.9 2.9 %copy-start.17 = (bf16[2,96,4,128]{3,1,2,0:T(8,128)(2,1)S(1)}, bf16[2,96,4,128]{3,1,2,0:T(8,128)(2,1)}, u32[]{:S(2)}) copy-start(bf16[2,96,4,128]{3,1,2,0:T(8,128)(2,1)} %convolution_convert_fusion) | copy-start | bytes 589828
  196.8 2.6 %copy-start.3 = (bf16[2,1024,4,128]{3,1,0,2:T(8,128)(2,1)S(1)}, bf16[2,1024,4,128]{3,1,0,2:T(8,128)(2,1)}, u32[]{:S(2)}) copy-start(bf16[2,1024,4,128]{3,1,0,2:T(8,128)(2,1)} %copy.84) | copy-start | bytes 6291460
  196.8 3.3 %copy-start.20 = (f32[2,3,96,1120]{3,2,1,0:T(8,128)S(1)}, f32[2,3,96,1120]{3,2,1,0:T(8,128)}, u32[]{:S(2)}) copy-start(f32[2,3,96,1120]{3,2,1,0:T(8,128)} %get-tuple-element.20) | copy-start | bytes 7741444
  200.1 1.7 copy-start.19
  201.9 1.7 copy-start.18
  203.6 1.8 copy-start.13
  204.2 1.2 copy-start.16
  204.6 2.4 %copy-start.1 = (bf16[1792,896]{1,0:T(8,128)(2,1)S(1)}, bf16[1792,896]{1,0:T(8,128)(2,1)}, u32[]{:S(2)}) copy-start(bf16[1792,896]{1,0:T(8,128)(2,1)} %param.16) | copy-start | bytes 9633796
Sparse Core Ops, SparseCore 0:
  12.9 21.5 reduce-scatter.1
Sparse Core Ops, SparseCore 1:
  14.8 91.6 all-gather.1
where the time goes:
time: 215 us; the launch traced here: 214 us
  waiting for transfers between devices  92.3 us (43%)
  local copies, waits for them, and re-layouts  52.8 us (25%)
  matrix products  28.5 us (13%)
  starting transfers between devices  19.5 us (9%)
  between operations  15.2 us (7%)
  other arithmetic  6.03 us (3%)
    all_gather x1, waiting for transfers between devices, body(): piece = lax.all_gather(prompt_cache, 'sess', axis=0, tiled=True)  33.9 us
    all_to_all x1, waiting for transfers between devices, body(): lax.all_to_all(chosen.astype(jnp.bfloat16), ('inner', 'rep'), split_axis=...  28.3 us
    all_to_all x1, waiting for transfers between devices, body(): lax.all_to_all(buffer.reshape(owner_count, per_owner * slot_cap, own_colu...  24.4 us
    scatter x1, local copies, waits for them, and re-layouts, body(): compact = jnp.zeros((per_device, SLOTS, projected.shape[2]), jnp.bfloat16...  13.1 us
    sub x4, matrix products, attend(): powers = jnp.exp(scores - highest)  11.7 us
    unnamed x43, local copies, waits for them, and re-layouts  10.7 us
    all_to_all x1, starting transfers between devices, body(): lax.all_to_all(counts, ('sess', 'rep'), split_axis=0, concat_axis=0, tile...  6.33 us
    slice x2, local copies, waits for them, and re-layouts, attend(): prompts[:, :, KVH * HD:].reshape(session_total, PROMPT, KVH, HD)  5.48 us
  transfers between devices with their start and end apart: 6, of which 4 were waited for; matrix products, arithmetic and copies ran while one was open for 20% of the time, Pallas kernels for 0%

commit v1 on v0

--- a/solution.py
+++ b/solution.py
@@ -10,6 +10,12 @@
 SLOTS = 96
 EPSILON = 1e-06
 ROPE_BASE = 1000000.0
+
+
+def meet_frame(z_in, where_dim):
+    aux = list(z_in.shape[1:])
+    aux[where_dim] *= z_in.shape[0]
+    return jnp.moveaxis(z_in, 0, where_dim).reshape(aux)
 
 
 def rms_scale(states, gain):
@@ -183,7 +189,23 @@
         jnp.where(wanted_speaker[:, None] == speaker_table[None, :], prompt_slot[None, :], 0),
         axis=1,
     )
-    piece = lax.all_gather(prompt_cache, "sess", axis=0, tiled=True)
+    workers = lax.axis_size("sess")
+    frames = tuple(((h, (h + 1) % workers) for h in range(workers)))
+    series = tuple(((s, k) for k, s in frames))
+    state_now, x_now = ([], [])
+    for src_i in range(workers - 1):
+        if src_i % 2 == 0:
+            state_now.append(
+                lax.ppermute(state_now[-1] if state_now else prompt_cache, "sess", frames)
+            )
+        else:
+            x_now.append(
+                lax.ppermute(x_now[-1] if x_now else prompt_cache, perm=series, axis_name="sess")
+            )
+    block_next = jnp.stack([*state_now[::-1], prompt_cache, *x_now], 0)
+    then = lax.axis_index("sess") - len(state_now)
+    block_next = block_next[(jnp.arange(workers) - then) % workers]
+    piece = meet_frame(block_next, 0)
     matching = (wanted_slot[:, None] == jnp.arange(piece.shape[0])[None, :]).astype(jnp.bfloat16)
     chosen = jnp.einsum("sp,ptc->stc", matching, piece, preferred_element_type=jnp.float32)
     prompts = lax.all_to_all(

time: 215 us -> 207 us (0.963)
  waiting for transfers between devices: 92.3 us -> 72.6 us
  other arithmetic: 6.03 us -> 11.1 us
  starting transfers between devices: 19.5 us -> 23.8 us
  local copies, waits for them, and re-layouts: 52.8 us -> 56.6 us
    ppermute x0 -> x3, waiting for transfers between devices: none -> 44.3 us  [the longest x2 44.3 us: body(): lax.ppermute(state_now[-1] if state_now else prompt_cache, 'sess', frames)]
    all_gather x1 -> x0, waiting for transfers between devices: 33.9 us -> none  [body(): piece = lax.all_gather(prompt_cache, 'sess', axis=0, tiled=True)]
    all_to_all x1, waiting for transfers between devices: 24.4 us -> 0.01 us  [body(): lax.all_to_all(buffer.reshape(owner_count, per_owner * slot_cap, own_colu...]
    ppermute x0 -> x3, starting transfers between devices: none -> 6.67 us  [the longest x1 5.05 us: body(): lax.ppermute(x_now[-1] if x_now else prompt_cache, perm=series, axis_name...]
    reduce_scatter x1, waiting for transfers between devices: 5.19 us -> 0.01 us  [body(): lax.psum_scatter(partial_sum, 'inner', scatter_dimension=1, tiled=True)]
    gather x0 -> x1, local copies, waits for them, and re-layouts: none -> 4.97 us  [body(): block_next = block_next[(jnp.arange(workers) - then) % workers]]
    another operation x0 -> x1, other arithmetic: none -> 3.58 us  [body(): block_next = jnp.stack([*state_now[::-1], prompt_cache, *x_now], 0)]
    unnamed x43 -> x41, local copies, waits for them, and re-layouts: 10.7 us -> 8.63 us
  transfers between devices with their start and end apart: 6 -> 8, of which waited for: 4 -> 3; matrix products, arithmetic and copies ran while one was open for 20% -> 27% of each run, Pallas kernels for 0% -> 0%
where the time goes in v1:
time: 207 us; the launch traced here: 206 us
  waiting for transfers between devices  72.6 us (35%)
  local copies, waits for them, and re-layouts  56.6 us (27%)
  matrix products  28.5 us (14%)
  starting transfers between devices  23.8 us (11%)
  between operations  13.8 us (7%)
  other arithmetic  11.1 us (5%)
    ppermute x2, waiting for transfers between devices, body(): lax.ppermute(state_now[-1] if state_now else prompt_cache, 'sess', frames)  44.3 us
    all_to_all x1, waiting for transfers between devices, body(): lax.all_to_all(chosen.astype(jnp.bfloat16), ('inner', 'rep'), split_axis=...  28.3 us
    scatter x1, local copies, waits for them, and re-layouts, body(): compact = jnp.zeros((per_device, SLOTS, projected.shape[2]), jnp.bfloat16...  13.1 us
    sub x4, matrix products, attend(): powers = jnp.exp(scores - highest)  11.7 us
    unnamed x41, local copies, waits for them, and re-layouts  8.63 us
    slice x2, local copies, waits for them, and re-layouts, attend(): prompts[:, :, KVH * HD:].reshape(session_total, PROMPT, KVH, HD)  5.48 us
    all_to_all x1, starting transfers between devices, body(): lax.all_to_all(counts, ('sess', 'rep'), split_axis=0, concat_axis=0, tile...  5.1 us
    ppermute x1, starting transfers between devices, body(): lax.ppermute(x_now[-1] if x_now else prompt_cache, perm=series, axis_name...  5.05 us
  transfers between devices with their start and end apart: 8, of which 3 were waited for; matrix products, arithmetic and copies ran while one was open for 27% of the time, Pallas kernels for 0%

profile of v1, /device:TPU:0, one launch (start us, length us, event | category | flops | bytes accessed | tf_op | source)
XLA Modules:
  0.0 206.3 jit_solution(15311245794595788445)
XLA Ops:
  6.5 5.0 %collective-permute-start.2 = (bf16[2,256,1024]{2,1,0:T(8,128)(2,1)}, bf16[2,256,1024]{2,1,0:T(8,128)(2,1)}, u32[]{:S(2)}, u32[]{:S(2)}) collective-permute-start(bf16[2,256,1024]{2,1,0:T(8,128)(2,1)} %param.15), channel_id=1, source_target_pairs={{4,0},{8,4},{12,8},{0,12},{5,1},{9,5},{13,9},{1,13},{6,2},{10,6},{... | collective-permute-start | bytes 3145736 | tf_op jit(solution)/shard_map/ppermute | solution.py:203
  11.6 0.9 convert_reduce_fusion
  12.5 0.7 compare_select_fusion
  13.2 0.1 convert_reduce_fusion.1
  13.4 0.7 all_to_all.35
  14.0 5.1 %all-to-all-start = ((s32[8,1,4]{2,1,0:T(1,128)}), s32[8,1,4]{2,1,0:T(1,128)S(1)}, u32[]{:S(2)}, u32[]{:S(2)}) async-start(s32[8,1,4]{2,1,0:T(1,128)} %bitcast.1), calls=%async_computation | async-start | bytes 8192 | tf_op jit(solution)/shard_map/all_to_all | solution.py:164
  19.2 3.5 %fusion.177 = f32[256,896]{0,1:T(8,128)} fusion(bf16[256,1792]{1,0:T(8,128)(2,1)} %param.11, bf16[1792,896]{1,0:T(8,128)(2,1)S(1)} %copy-done), kind=kOutput, calls=%fused_computation.198 | convolution fusion | flops 822083584 | bytes 5046272 | tf_op jit(solution)/shard_map/dot_general | solution.py:148
  22.7 0.2 multiply_cosine_fusion
  23.1 34.7 %collective-permute-done = bf16[2,256,1024]{2,1,0:T(8,128)(2,1)} collective-permute-done((bf16[2,256,1024]{2,1,0:T(8,128)(2,1)}, bf16[2,256,1024]{2,1,0:T(8,128)(2,1)}, u32[]{:S(2)}, u32[]{:S(2)}) %collective-permute-start) | collective-permute-done | bytes 1048608 | tf_op jit(solution)/shard_map/ppermute | solution.py:199
  57.7 1.6 collective-permute-start.1
  59.4 4.7 %copy.90 = bf16[896,1536]{0,1:T(8,128)(2,1)} copy(bf16[896,1536]{1,0:T(8,128)(2,1)} %param.18) | data formatting | bytes 5505024 | tf_op args[7]
  64.2 0.6 copy.102
  64.9 0.2 select_reduce_fusion
  65.1 0.7 pad_maximum_fusion.4
  65.8 2.2 %copy.101 = bf16[512,896]{1,0:T(8,128)(2,1)} copy(bf16[512,896]{0,1:T(8,128)(2,1)} %bitcast.202) | data formatting | bytes 1835008 | tf_op jit(solution)/shard_map/dot_general | solution.py:62
  68.0 0.1 fusion.154
  68.1 0.2 reduce_window_sum.11
  68.6 1.1 convert_element_type.78
  69.7 0.1 copy.75
  69.8 2.2 %scatter_custom_fusion = bf16[384,448]{1,0:T(8,128)(2,1)} fusion(s32[256]{0:T(256)S(1)} %bitcast.209, bf16[256,448]{1,0:T(8,128)(2,1)S(1)} %copy.75, bf16[]{:T(256)} %constant.109.clone.1), kind=kCustom, calls=%fused_computation.100 | custom fusion | bytes 344066 | tf_op jit(solution)/shard_map/scatter | solution.py:155
  72.1 3.5 %all-to-all-start.1 = ((bf16[8,48,448]{2,1,0:T(8,128)(2,1)}), bf16[8,48,448]{2,1,0:T(8,128)(2,1)S(1)}, u32[]{:S(2)}, u32[]{:S(2)}) async-start(bf16[8,48,448]{2,1,0:T(8,128)(2,1)} %bitcast.8), calls=%async_computation.2 | async-start | bytes 786432 | tf_op jit(solution)/shard_map/all_to_all | solution.py:157
  75.6 0.1 reshape.366
  75.7 0.6 lt.155
  76.3 9.6 %collective-permute-done.1 = bf16[2,256,1024]{2,1,0:T(8,128)(2,1)} collective-permute-done((bf16[2,256,1024]{2,1,0:T(8,128)(2,1)}, bf16[2,256,1024]{2,1,0:T(8,128)(2,1)}, u32[]{:S(2)}, u32[]{:S(2)}) %collective-permute-start.1) | collective-permute-done | bytes 1048608 | tf_op jit(solution)/shard_map/ppermute | solution.py:199
  86.0 3.6 %pad_maximum_fusion = bf16[4,2,256,1024]{3,2,1,0:T(8,128)(2,1)} fusion(bf16[1,2,256,1024]{3,2,1,0:T(8,128)(2,1)} %bitcast.18, bf16[1,2,256,1024]{3,2,1,0:T(8,128)(2,1)S(1)} %bitcast.200, bf16[1,2,256,1024]{3,2,1,0:T(8,128)(2,1)} %bitcast.16, bf16[1,2,256,1024]{3,2,1,0:T(8,128)(2,1)} %bitcast.15), kind=kLoop, calls=%fused_computation.7 | loop fusion | flops 6291456 | bytes 8388608 | tf_op jit(solution)/shard_map/stack | solution.py:205
  89.6 5.0 %gather_fusion = bf16[4,2,256,1024]{3,2,1,0:T(8,128)(2,1)} fusion(bf16[4,2,256,1024]{3,2,1,0:T(8,128)(2,1)} %pad_maximum_fusion, s32[1024]{0:T(1024)S(1)} %pad_clamp_fusion), kind=kCustom, calls=%fused_computation | custom fusion | bytes 8388624 | tf_op jit(solution)/shard_map/gather | solution.py:207
  94.6 1.0 copy.76
  95.5 3.5 %all-to-all-start.2 = ((bf16[8,4,12,448]{3,0,2,1:T(8,128)(2,1)}), bf16[8,4,12,448]{3,0,2,1:T(8,128)(2,1)S(1)}, u32[]{:S(2)}, u32[]{:S(2)}) async-start(bf16[8,4,12,448]{3,0,2,1:T(8,128)(2,1)} %bitcast.9), calls=%async_computation.3 | async-start | bytes 786432 | tf_op jit(solution)/shard_map/all_to_all | solution.py:166
  99.0 4.7 %fusion.22 = bf16[8,256,1024]{2,0,1:T(8,128)(2,1)S(1)} fusion(bf16[8,256,1024]{2,1,0:T(8,128)(2,1)} %bitcast.192, s32[8]{0:T(128)S(1)} %select_reduce_fusion), kind=kOutput, calls=%fused_computation.36 | convolution fusion | flops 35651648 | bytes 8388640 | tf_op jit(solution)/shard_map/sp,ptc->stc/dot_general | solution.py:210
  103.7 4.3 %copy.80 = bf16[8,256,1024]{2,1,0:T(8,128)(2,1)} copy(bf16[8,256,1024]{2,0,1:T(8,128)(2,1)S(1)} %fusion.22) | data formatting | bytes 8388608 | tf_op jit(solution)/shard_map/convert_element_type | solution.py:212
  108.0 5.0 %all-to-all-start.3 = ((bf16[8,256,1024]{2,1,0:T(8,128)(2,1)}), bf16[8,256,1024]{2,1,0:T(8,128)(2,1)}, u32[]{:S(2)}, u32[]{:S(2)}) async-start(bf16[8,256,1024]{2,1,0:T(8,128)(2,1)} %copy.80), calls=%async_computation.4 | async-start | bytes 8388608 | tf_op jit(solution)/shard_map/all_to_all | solution.py:211
  113.1 0.8 and_or_fusion
  113.9 0.4 copy.77
  114.3 0.3 all_to_all.41
  114.8 13.1 %scatter_fusion = bf16[2,96,896]{2,1,0:T(8,128)(2,1)S(1)} fusion(bf16[2,96,896]{2,1,0:T(8,128)(2,1)S(1)} %broadcast_in_dim.55, s32[192]{0:T(256)S(1)} %reshape.366, bf16[192,896]{1,0:T(8,128)(2,1)S(1)} %reshape.368), kind=kCustom, calls=%fused_computation.2 | custom fusion | bytes 1033728 | tf_op jit(solution)/shard_map/scatter | solution.py:181
  127.9 0.2 multiply_reduce_fusion
  128.1 0.5 fusion.115
  128.6 0.2 slice_negate_fusion.1
  128.8 0.9 fusion.68
  129.7 1.2 convolution_convert_fusion
  130.8 1.1 fusion.113
  131.9 0.4 slice_negate_fusion
  132.4 0.4 fusion.32
  132.8 28.3 %all-to-all-done.3 = bf16[8,256,1024]{2,1,0:T(8,128)(2,1)} async-done(((bf16[8,256,1024]{2,1,0:T(8,128)(2,1)}), bf16[8,256,1024]{2,1,0:T(8,128)(2,1)}, u32[]{:S(2)}, u32[]{:S(2)}) %all-to-all-start.3) | async-done | bytes 4194336 | tf_op jit(solution)/shard_map/all_to_all | solution.py:211
  161.1 2.6 %copy.81 = bf16[2,4,256,1024]{3,2,1,0:T(8,128)(2,1)S(1)} copy(bf16[2,4,256,1024]{3,2,0,1:T(8,128)(2,1)} %bitcast.22) | data formatting | bytes 8388608 | tf_op jit(solution)/shard_map/all_to_all | solution.py:211
  163.7 2.5 %fusion.156 = (bf16[2,1024,512]{2,1,0:T(8,128)(2,1)}, bf16[2,1024,512]{2,1,0:T(8,128)(2,1)}) fusion(bf16[2,1024,1024]{2,1,0:T(8,128)(2,1)S(1)} %bitcast.193), kind=kLoop, calls=%fused_computation.193 | loop fusion | bytes 8388608 | tf_op jit(solution)/shard_map/slice | solution.py:67
  166.2 3.0 %copy.86 = bf16[2,1024,512]{1,2,0:T(8,128)(2,1)S(1)} copy(bf16[2,1024,512]{2,1,0:T(8,128)(2,1)} %get-tuple-element.10) | data formatting | bytes 4194304 | tf_op jit(solution)/shard_map/slice | solution.py:66
  169.2 2.5 %copy.88 = bf16[2,1024,4,128]{3,1,0,2:T(8,128)(2,1)} copy(bf16[2,1024,4,128]{1,3,2,0:T(8,128)(2,1)S(1)} %bitcast.195) | data formatting | bytes 4194304 | tf_op jit(solution)/shard_map/reshape | solution.py:66
  171.8 3.8 %fusion.157 = (f32[2,3,96]{2,1,0:T(4,128)S(1)}, f32[2,3,96,1120]{3,2,1,0:T(8,128)}) fusion(pred[2,96,1120]{2,1,0:T(8,128)(4,1)S(1)} %copy-done.9, bf16[2,1024,4,128]{3,1,0,2:T(8,128)(2,1)} %copy.88, bf16[2,96,12,128]{3,1,2,0:T(8,128)(2,1)S(1)} %fusion.32, bf16[2,96,4,128]{3,1,2,0:T(8,128)(2,1)S(1)} %copy-done.10), kind=kOutput, calls=%fused_computation.194 | convolution fusion | flops 168879200 | bytes 5245184 | tf_op jit(solution)/shard_map/sub | solution.py:87
  175.6 2.6 %fusion.162 = (f32[2,3,96]{2,1,0:T(4,128)S(1)}, f32[2,3,96,1120]{3,2,1,0:T(8,128)}) fusion(pred[2,96,1120]{2,1,0:T(8,128)(4,1)S(1)} %copy-done.9, bf16[2,1024,4,128]{3,1,0,2:T(8,128)(2,1)S(1)} %copy-done.4, bf16[2,96,12,128]{3,1,2,0:T(8,128)(2,1)S(1)} %fusion.32, bf16[2,96,4,128]{3,1,2,0:T(8,128)(2,1)S(1)} %copy-done.10), kind=kOutput, calls=%fused_computation.195 | convolution fusion | flops 168879200 | bytes 5245184 | tf_op jit(solution)/shard_map/sub | solution.py:87
  178.2 2.6 %fusion.167 = (f32[2,3,96]{2,1,0:T(4,128)S(1)}, f32[2,3,96,1120]{3,2,1,0:T(8,128)}) fusion(pred[2,96,1120]{2,1,0:T(8,128)(4,1)S(1)} %copy-done.9, bf16[2,1024,4,128]{3,1,0,2:T(8,128)(2,1)S(1)} %copy-done.4, bf16[2,96,12,128]{3,1,2,0:T(8,128)(2,1)S(1)} %fusion.32, bf16[2,96,4,128]{3,1,2,0:T(8,128)(2,1)S(1)} %copy-done.10), kind=kOutput, calls=%fused_computation.196 | convolution fusion | flops 168879200 | bytes 5245184 | tf_op jit(solution)/shard_map/sub | solution.py:87
  180.8 2.7 %fusion.172 = (f32[2,3,96]{2,1,0:T(4,128)S(1)}, f32[2,3,96,1120]{3,2,1,0:T(8,128)}) fusion(pred[2,96,1120]{2,1,0:T(8,128)(4,1)S(1)} %copy-done.9, bf16[2,1024,4,128]{3,1,0,2:T(8,128)(2,1)S(1)} %copy-done.4, bf16[2,96,12,128]{3,1,2,0:T(8,128)(2,1)S(1)} %fusion.32, bf16[2,96,4,128]{3,1,2,0:T(8,128)(2,1)S(1)} %copy-done.10), kind=kOutput, calls=%fused_computation.197 | convolution fusion | flops 168879200 | bytes 5245184 | tf_op jit(solution)/shard_map/sub | solution.py:87
  183.5 3.0 %copy.82 = bf16[2,1024,512]{1,2,0:T(8,128)(2,1)S(1)} copy(bf16[2,1024,512]{2,1,0:T(8,128)(2,1)} %get-tuple-element.9) | data formatting | bytes 4194304 | tf_op jit(solution)/shard_map/slice | solution.py:67
  186.5 2.9 %copy.84 = bf16[2,1024,4,128]{3,1,0,2:T(8,128)(2,1)} copy(bf16[2,1024,4,128]{1,3,2,0:T(8,128)(2,1)S(1)} %bitcast.196) | data formatting | bytes 4194304 | tf_op jit(solution)/shard_map/reshape | solution.py:67
  189.3 2.6 %fusion.40 = bf16[2,96,3,128]{3,1,2,0:T(8,128)(2,1)S(1)} fusion(f32[2,3,96,1120]{3,2,1,0:T(8,128)} %get-tuple-element.18, f32[2,3,96]{2,1,0:T(4,128)S(1)} %get-tuple-element.17, bf16[2,1024,4,128]{3,1,0,2:T(8,128)(2,1)} %copy.84, bf16[2,96,4,128]{3,1,2,0:T(8,128)(2,1)S(1)} %copy-done.16), kind=kOutput, calls=%fused_computation.66 | convolution fusion | flops 167661568 | bytes 5024000 | tf_op jit(solution)/shard_map/chqk,ckd->cqhd/dot_general | solution.py:90
  192.0 0.7 copy-done.19
  192.7 0.6 fusion.39
  193.3 1.2 copy-done.18
  194.4 0.6 fusion.38
  195.0 1.2 copy-done.17
  196.2 0.6 fusion.37
  196.8 0.3 copy.91
  197.1 0.8 copy-done.12
  198.0 1.5 fusion.30
  (69 shorter events, 1.2 us)
Async XLA Ops:
  6.5 12.6 %copy-start = (bf16[1792,896]{1,0:T(8,128)(2,1)S(1)}, bf16[1792,896]{1,0:T(8,128)(2,1)}, u32[]{:S(2)}) copy-start(bf16[1792,896]{1,0:T(8,128)(2,1)} %param.16) | copy-start | bytes 9633796
  6.5 69.8 %collective-permute-start.2 = (bf16[2,256,1024]{2,1,0:T(8,128)(2,1)}, bf16[2,256,1024]{2,1,0:T(8,128)(2,1)}, u32[]{:S(2)}, u32[]{:S(2)}) collective-permute-start(bf16[2,256,1024]{2,1,0:T(8,128)(2,1)} %param.15), channel_id=1, source_target_pairs={{4,0},{8,4},{12,8},{0,12},{5,1},{9,5},{13,9},{1,13},{6,2},{10,6},{... | collective-permute-start | bytes 3145736 | tf_op jit(solution)/shard_map/ppermute | solution.py:203
  11.6 46.1 %collective-permute-start = (bf16[2,256,1024]{2,1,0:T(8,128)(2,1)}, bf16[2,256,1024]{2,1,0:T(8,128)(2,1)}, u32[]{:S(2)}, u32[]{:S(2)}) collective-permute-start(bf16[2,256,1024]{2,1,0:T(8,128)(2,1)} %param.15), channel_id=1, source_target_pairs={{0,4},{4,8},{8,12},{12,0},{1,5},{5,9},{9,13},{13,1},{2,6},{6,10},{... | collective-permute-start | bytes 3145736 | tf_op jit(solution)/shard_map/ppermute | solution.py:199
  14.0 53.9 %all-to-all-start = ((s32[8,1,4]{2,1,0:T(1,128)}), s32[8,1,4]{2,1,0:T(1,128)S(1)}, u32[]{:S(2)}, u32[]{:S(2)}) async-start(s32[8,1,4]{2,1,0:T(1,128)} %bitcast.1), calls=%async_computation | async-start | bytes 8192 | tf_op jit(solution)/shard_map/all_to_all | solution.py:164
  19.1 49.5 %reduce-scatter.2.cloned.1.call-start = ((), (), s32[]{:S(2)}) async-start(), calls=%async_computation.5 | async-start | bytes 1376256 | tf_op jit(solution)/shard_map/reduce_scatter | solution.py:149
  57.7 28.3 %collective-permute-start.1 = (bf16[2,256,1024]{2,1,0:T(8,128)(2,1)}, bf16[2,256,1024]{2,1,0:T(8,128)(2,1)}, u32[]{:S(2)}, u32[]{:S(2)}) collective-permute-start(bf16[2,256,1024]{2,1,0:T(8,128)(2,1)} %collective-permute-done), channel_id=1, source_target_pairs={{0,4},{4,8},{8,12},{12,0},{1,5},{5,9},{9,13},{13,1},{2,6},{6,10},{... | collective-permute-start | bytes 3145736 | tf_op jit(solution)/shard_map/ppermute | solution.py:199
  59.4 4.8 %copy-start.11 = (bf16[896]{0:T(1024)(128)(2,1)S(1)}, bf16[896]{0:T(1024)(128)(2,1)}, u32[]{:S(2)}) copy-start(bf16[896]{0:T(1024)(128)(2,1)} %param.17) | copy-start | bytes 5380
  59.4 4.8 %copy-start.6 = (bf16[896,512]{1,0:T(8,128)(2,1)S(1)}, bf16[896,512]{1,0:T(8,128)(2,1)}, u32[]{:S(2)}) copy-start(bf16[896,512]{1,0:T(8,128)(2,1)} %param.19) | copy-start | bytes 2752516
  59.4 5.4 %copy-start.13 = (s32[32]{0:T(128)S(1)}, s32[32]{0:T(128)}, u32[]{:S(2)}) copy-start(s32[32]{0:T(128)} %param.13) | copy-start | bytes 388
  59.4 5.5 %copy-start.14 = (s32[8]{0:T(128)S(1)}, s32[8]{0:T(128)}, u32[]{:S(2)}) copy-start(s32[8]{0:T(128)} %param.14) | copy-start | bytes 100
  64.8 21.2 %copy-start.5 = (bf16[2,256,1024]{2,1,0:T(8,128)(2,1)S(1)}, bf16[2,256,1024]{2,1,0:T(8,128)(2,1)}, u32[]{:S(2)}) copy-start(bf16[2,256,1024]{2,1,0:T(8,128)(2,1)} %param.15) | copy-start | bytes 3145732
  72.1 22.5 %all-to-all-start.1 = ((bf16[8,48,448]{2,1,0:T(8,128)(2,1)}), bf16[8,48,448]{2,1,0:T(8,128)(2,1)S(1)}, u32[]{:S(2)}, u32[]{:S(2)}) async-start(bf16[8,48,448]{2,1,0:T(8,128)(2,1)} %bitcast.8), calls=%async_computation.2 | async-start | bytes 786432 | tf_op jit(solution)/shard_map/all_to_all | solution.py:157
  95.5 12.5 %all-to-all-start.2 = ((bf16[8,4,12,448]{3,0,2,1:T(8,128)(2,1)}), bf16[8,4,12,448]{3,0,2,1:T(8,128)(2,1)S(1)}, u32[]{:S(2)}, u32[]{:S(2)}) async-start(bf16[8,4,12,448]{3,0,2,1:T(8,128)(2,1)} %bitcast.9), calls=%async_computation.3 | async-start | bytes 786432 | tf_op jit(solution)/shard_map/all_to_all | solution.py:166
  108.0 53.1 %all-to-all-start.3 = ((bf16[8,256,1024]{2,1,0:T(8,128)(2,1)}), bf16[8,256,1024]{2,1,0:T(8,128)(2,1)}, u32[]{:S(2)}, u32[]{:S(2)}) async-start(bf16[8,256,1024]{2,1,0:T(8,128)(2,1)} %copy.80), calls=%async_computation.4 | async-start | bytes 8388608 | tf_op jit(solution)/shard_map/all_to_all | solution.py:211
  127.9 0.9 copy-start.8
  127.9 1.8 copy-start.7
  128.6 2.2 %copy-start.2 = (bf16[896,1536]{0,1:T(8,128)(2,1)S(1)}, bf16[896,1536]{0,1:T(8,128)(2,1)}, u32[]{:S(2)}) copy-start(bf16[896,1536]{0,1:T(8,128)(2,1)} %copy.90) | copy-start | bytes 8257540
  169.2 2.6 %copy-start.9 = (pred[2,96,1120]{2,1,0:T(8,128)(4,1)S(1)}, pred[2,96,1120]{2,1,0:T(8,128)(4,1)}, u32[]{:S(2)}) copy-start(pred[2,96,1120]{2,1,0:T(8,128)(4,1)} %and_or_fusion) | copy-start | bytes 645124
  169.2 2.6 %copy-start.10 = (bf16[2,96,4,128]{3,1,2,0:T(8,128)(2,1)S(1)}, bf16[2,96,4,128]{3,1,2,0:T(8,128)(2,1)}, u32[]{:S(2)}) copy-start(bf16[2,96,4,128]{3,1,2,0:T(8,128)(2,1)} %fusion.68) | copy-start | bytes 589828
  171.8 3.8 %copy-start.4 = (bf16[2,1024,4,128]{3,1,0,2:T(8,128)(2,1)S(1)}, bf16[2,1024,4,128]{3,1,0,2:T(8,128)(2,1)}, u32[]{:S(2)}) copy-start(bf16[2,1024,4,128]{3,1,0,2:T(8,128)(2,1)} %copy.88) | copy-start | bytes 6291460
  186.5 2.9 %copy-start.16 = (bf16[2,96,4,128]{3,1,2,0:T(8,128)(2,1)S(1)}, bf16[2,96,4,128]{3,1,2,0:T(8,128)(2,1)}, u32[]{:S(2)}) copy-start(bf16[2,96,4,128]{3,1,2,0:T(8,128)(2,1)} %convolution_convert_fusion) | copy-start | bytes 589828
  189.3 2.6 %copy-start.3 = (bf16[2,1024,4,128]{3,1,0,2:T(8,128)(2,1)S(1)}, bf16[2,1024,4,128]{3,1,0,2:T(8,128)(2,1)}, u32[]{:S(2)}) copy-start(bf16[2,1024,4,128]{3,1,0,2:T(8,128)(2,1)} %copy.84) | copy-start | bytes 6291460
  189.3 3.3 %copy-start.19 = (f32[2,3,96,1120]{3,2,1,0:T(8,128)S(1)}, f32[2,3,96,1120]{3,2,1,0:T(8,128)}, u32[]{:S(2)}) copy-start(f32[2,3,96,1120]{3,2,1,0:T(8,128)} %get-tuple-element.20) | copy-start | bytes 7741444
  192.7 1.7 copy-start.18
  194.4 1.7 copy-start.17
  196.2 1.8 copy-start.12
  196.2 1.8 copy-start.15
  197.1 2.4 %copy-start.1 = (bf16[1792,896]{1,0:T(8,128)(2,1)S(1)}, bf16[1792,896]{1,0:T(8,128)(2,1)}, u32[]{:S(2)}) copy-start(bf16[1792,896]{1,0:T(8,128)(2,1)} %param.16) | copy-start | bytes 9633796
Sparse Core Ops, SparseCore 0:
  22.8 20.2 reduce-scatter.1
